TPU v7x, 128 devices: a whole 4x4x4 slice. The times are simulated.
128 devices in a mesh: group: 4 (over x), bulk: 32 (over z, y, core).
Axes of the slice: x: 4, y: 4, z: 4, core: 2. Of those that a mesh axis runs over, the one named last changes fastest.
Arguments:
- rhs: float32 [512, 64, 128], P(('group', 'bulk')), may hold values from -90 to 90, as said below
- diag_tiles: float32 [512, 128, 128], P(('group', 'bulk')), may hold values from -0.06 to 0.06
- offdiag_blocks: float32 [512, 11, 128, 128], P(('group', 'bulk')), may hold values from -0.026 to 0.026
- coupling: float32 [256, 4, 128, 128], P(('group', 'bulk')), may hold values from -0.05 to 0.05, as said below
- col_index: int32 [512, 11], replicated, may hold values from 0 to 511, as said below
- load: int32 [512], replicated, may hold values from 3 to 11
- new_slot: int32 [512], replicated, may hold values from 0 to 511, as said below
Outputs:
- solution_out: float32 [512, 64, 128], P(('group', 'bulk'))
- residual_out: float32 [512, 64, 128], P(('group', 'bulk'))
Inputs may be any that keep to these rules, and one draw needn't show every extreme that they name: `rhs`: made of random entries times scales of the rows and of the columns. `coupling`: entry [d * 2 + k, h] is the transpose of entry [(h * 32 + d % 32) * 2 + k, d // 32]. `col_index`: for each part g and each tile position t, the column t of the 128 block rows of part g is a permutation of that part's slots g * 128 to (g + 1) * 128 - 1. Of the 44 entries of the 4 block rows of one device (slots d * 4 to (d + 1) * 4 - 1), at most 2 name slots of any one device, and exactly 2 name slots of some device. `new_slot`: A permutation. On every device exactly one block row moves, from a slot k with 2 <= k % 4; it stays in its part, goes from owner b to owner b XOR m, where m (1 to 31) is one number for the whole part, and takes the slot that the moving row of that device leaves.
All inputs are finite; a program needn't handle non-finite values.
Results may differ from a plain program's by a relative error of at most 0.0003.
Values sent between devices are 32-bit elements; how exact they have to be, the bound alone decides.
A program may use at most 64 MiB of HBM per device.

v0:
```python
import jax
import jax.numpy as jnp
from jax import lax
from jax.sharding import PartitionSpec as P

highest = lax.Precision.HIGHEST
diagonal_shift = 4.0


def from_partner(value, axis, bit):
    mask = 2**bit
    pairs = [(source, source ^ mask) for source in range(lax.axis_size(axis))]
    return lax.ppermute(value, axis, pairs)


def chol_apply(matrix, right):
    factor = jnp.linalg.cholesky(matrix)
    middle = lax.linalg.triangular_solve(factor, right, left_side=True, lower=True)
    return lax.linalg.triangular_solve(factor, middle, left_side=True, lower=True, transpose_a=True)


def global_gram(left, right):
    partial_gram = jnp.einsum("snt,smt->nm", left, right, precision=highest)
    total = lax.psum(partial_gram, ("group", "bulk"))
    return 0.5 * (total + total.T)


def operate(vectors, diag, masked, column_ids, coupling):
    row_count = vectors.shape[0]
    boundary_rows = coupling.shape[0]
    part_count = coupling.shape[1]
    group_rows = row_count * lax.axis_size("bulk")
    border = lax.all_gather(vectors[:boundary_rows], "group", axis=0, tiled=True)
    final_output = diagonal_shift * vectors + jnp.einsum(
        "rnj,rij->rni", vectors, diag, precision=highest
    )
    returned = jnp.einsum("rni,rkij->rknj", vectors, masked, precision=highest)
    flat_terms = returned.reshape((-1,) + vectors.shape[1:])
    panel = lax.all_gather(vectors, "bulk", axis=0, tiled=True)
    buffer = jax.ops.segment_sum(flat_terms, column_ids.reshape(-1), num_segments=group_rows)
    owed = lax.psum_scatter(buffer, "bulk", scatter_dimension=0, tiled=True)
    picked = panel[column_ids]
    final_output = (
        final_output + jnp.einsum("rknj,rkij->rni", picked, masked, precision=highest) + owed
    )
    border = border.reshape((part_count, boundary_rows) + vectors.shape[1:])
    crossed = jnp.einsum("khij,hknj->kni", coupling, border, precision=highest)
    return final_output.at[:boundary_rows].add(crossed)


def advance(state, diag, masked, column_ids, coupling, last_step):
    solution, resid, direction, gram_rr = state
    image = operate(direction, diag, masked, column_ids, coupling)
    gram_pq = global_gram(direction, image)
    alpha = chol_apply(gram_pq, gram_rr)
    solution = solution + jnp.einsum("mn,smt->snt", alpha, direction, precision=highest)
    resid = resid - jnp.einsum("mn,smt->snt", alpha, image, precision=highest)
    if not last_step:
        gram_new = global_gram(resid, resid)
        beta = chol_apply(gram_rr, gram_new)
        direction = resid + jnp.einsum("mn,smt->snt", beta, direction, precision=highest)
        gram_rr = gram_new
    return (solution, resid, direction, gram_rr)


def local(rhs, diag_tiles, offdiag_blocks, coupling, col_index, load, new_slot):
    row_count = rhs.shape[0]
    off_count = offdiag_blocks.shape[1]
    bulk_count = lax.axis_size("bulk")
    group_rows = row_count * bulk_count
    my_group = lax.axis_index("group")
    my_bulk = lax.axis_index("bulk")
    first_slot = (my_group * bulk_count + my_bulk) * row_count
    group_base = my_group * group_rows
    own_slots = first_slot + jnp.arange(row_count, dtype=jnp.int32)
    tile_ids = jnp.arange(off_count, dtype=jnp.int32)
    old_columns = col_index[own_slots] - group_base
    old_mask = (tile_ids[None, :] < load[own_slots][:, None]).astype(jnp.float32)
    old_masked = offdiag_blocks * old_mask[:, :, None, None]
    own_new = new_slot[own_slots]
    leaving = jnp.argmax((own_new != own_slots).astype(jnp.int32))
    target = own_new[leaving]
    target_bulk = target // row_count % bulk_count
    xor_mask = jnp.bitwise_xor(target_bulk, my_bulk)
    start_state = (jnp.zeros_like(rhs), rhs, rhs, global_gram(rhs, rhs))
    state = advance(start_state, diag_tiles, old_masked, old_columns, coupling, False)
    solution, resid, direction, gram_rr = state
    pieces = [
        offdiag_blocks[leaving],
        diag_tiles[leaving],
        solution[leaving],
        resid[leaving],
        direction[leaving],
    ]
    flat = jnp.concatenate([piece.reshape(-1) for piece in pieces])
    for bit_pos in range(bulk_count.bit_length() - 1):
        partner = from_partner(flat, "bulk", bit_pos)
        chosen = jnp.bitwise_and(jnp.right_shift(xor_mask, bit_pos), 1) == 1
        flat = jnp.where(chosen, partner, flat)
    outputs = []
    offset = 0
    for piece in pieces:
        outputs.append(flat[offset : offset + piece.size].reshape(piece.shape))
        offset = offset + piece.size
    moved_off = offdiag_blocks.at[leaving].set(outputs[0])
    moved_diag = diag_tiles.at[leaving].set(outputs[1])
    solution = solution.at[leaving].set(outputs[2])
    resid = resid.at[leaving].set(outputs[3])
    direction = direction.at[leaving].set(outputs[4])
    inverse = (
        jnp.zeros_like(new_slot).at[new_slot].set(jnp.arange(new_slot.shape[0], dtype=jnp.int32))
    )
    old_rows = inverse[own_slots]
    new_columns = new_slot[col_index[old_rows]] - group_base
    new_mask = (tile_ids[None, :] < load[old_rows][:, None]).astype(jnp.float32)
    new_masked = moved_off * new_mask[:, :, None, None]
    state = advance(
        (solution, resid, direction, gram_rr), moved_diag, new_masked, new_columns, coupling, True
    )
    return (state[0], state[1])


def solution(mesh):
    return jax.shard_map(
        local,
        mesh=mesh,
        in_specs=(
            P(("group", "bulk"), None, None),
            P(("group", "bulk"), None, None),
            P(("group", "bulk"), None, None, None),
            P(("group", "bulk"), None, None, None),
            P(),
            P(),
            P(),
        ),
        out_specs=(P(("group", "bulk"), None, None), P(("group", "bulk"), None, None)),
        check_vma=False,
    )
```

profile of v0, /device:TPU:1, one launch (start us, length us, event | category | flops | bytes accessed | tf_op | source)
XLA Modules:
  0.0 662.4 jit_solution(1041182074401895514)
XLA Ops:
  7.3 1.9 copy.86
  9.9 1.6 copy.40
  12.1 2.6 scatter_custom_fusion.1
  15.9 1.5 gather_fusion
  18.7 2.2 gather_fusion.5
  25.3 3.2 fusion.4
  28.5 2.5 broadcast.320.clone
  31.0 8.0 %scatter_fusion = f32[128,64,128]{2,1,0:T(8,128)} fusion(f32[128,64,128]{2,1,0:T(8,128)} %broadcast.320.clone, s32[44]{0:T(128)} %reshape.516, f32[44,64,128]{2,1,0:T(8,128)} %bitcast.222), kind=kCustom, calls=%fused_computation.9 | custom fusion | flops 360448 | bytes 4325552 | tf_op jit(solution)/shard_map/scatter-add | solution.py:40
  40.2 1.3 fusion.68
  45.5 13.0 %all_gather.13 = f32[8,64,128]{2,1,0:T(8,128)} all-gather(f32[2,64,128]{2,1,0:T(8,128)} %slice.208), channel_id=1, replica_groups=mesh['group'=4,'bulk'=32] {'group'}, dimensions={0}, use_global_device_ids=true | all-gather | bytes 327680 | tf_op jit(solution)/shard_map/all_gather | solution.py:33
  60.9 1.5 bitcast_dynamic-update-slice_fusion
  62.4 4.0 gather_fusion.1
  66.4 5.4 fusion.12
  71.8 71.6 %reduce-scatter.3.cloned.1.call-done = f32[4,64,128]{2,1,0:T(8,128)} async-done(((f32[128,64,128]{2,1,0:T(8,128)}), f32[4,64,128]{2,1,0:T(8,128)}) %reduce-scatter.3.cloned.1.call-update) | async-done | bytes 131088 | tf_op jit(solution)/shard_map/reduce_scatter | solution.py:41
  143.4 1.7 fusion.21
  145.1 1.6 fusion.29
  148.2 66.3 %all-reduce = (f32[64,64]{1,0:T(8,128)}, f32[64,64]{1,0:T(8,128)}) all-reduce(f32[64,64]{1,0:T(8,128)} %convolution_bitcast_fusion.11, f32[64,64]{1,0:T(8,128)} %convolution_bitcast_fusion.12), channel_id=1, replica_groups=mesh['group'=4,'bulk'=32] {'group','bulk'}, use_global_device_ids=true, to_apply=%region_5.7 | all-reduce | flops 8192 | bytes 65536 | tf_op jit(solution)/shard_map/psum | solution.py:24
  214.6 1.4 copy.45
  216.0 1.4 fusion.56
  217.4 1.4 copy.48
  218.8 1.5 copy.43
  220.3 1.4 fusion.61
  221.7 1.4 copy.44
  223.1 1.4 fusion.60
  224.5 7.2 %cholesky.59 = f32[64,64]{1,0:T(8,128)} custom-call(f32[64,64]{1,0:T(8,128)} %fusion.60), custom_call_target="Cholesky" | custom-call | tf_op jit(solution)/shard_map/jit(cholesky)/cholesky | solution.py:17
  233.2 2.1 fusion.36
  235.3 6.3 custom-call.13
  243.6 1.8 fusion.25
  246.3 1.4 fusion.55
  247.7 7.2 %cholesky.70 = f32[64,64]{1,0:T(8,128)} custom-call(f32[64,64]{1,0:T(8,128)} %fusion.55), custom_call_target="Cholesky" | custom-call | tf_op jit(solution)/shard_map/jit(cholesky)/cholesky | solution.py:17
  256.4 2.1 fusion.37
  258.5 6.3 custom-call.15
  264.7 1.8 convolution_bitcast_fusion.9
  266.6 63.0 %psum.30 = f32[64,64]{1,0:T(8,128)} all-reduce(f32[64,64]{1,0:T(8,128)} %convolution_bitcast_fusion.9), channel_id=1, replica_groups=mesh['group'=4,'bulk'=32] {'group','bulk'}, use_global_device_ids=true, to_apply=%region_8.12 | all-reduce | flops 4096 | bytes 32768 | tf_op jit(solution)/shard_map/psum | solution.py:24
  329.6 1.4 copy.49
  334.2 1.4 bitcast_dynamic-update-slice_fusion.3
  335.6 1.4 bitcast_dynamic-update-slice_fusion.2
  341.3 2.2 broadcast_select_fusion
  344.7 20.3 %collective-permute-done.1 = f32[221184]{0:T(1024)} collective-permute-done((f32[221184]{0:T(1024)}, f32[221184]{0:T(1024)}, u32[]{:S(2)}, u32[]{:S(2)}) %collective-permute-start.1) | collective-permute-done | bytes 884768 | tf_op jit(solution)/shard_map/ppermute | solution.py:13
  365.0 2.2 broadcast_select_fusion.1
  367.2 2.9 collective-permute-start.2
  370.2 19.2 %collective-permute-done.2 = f32[221184]{0:T(1024)} collective-permute-done((f32[221184]{0:T(1024)}, f32[221184]{0:T(1024)}, u32[]{:S(2)}, u32[]{:S(2)}) %collective-permute-start.2) | collective-permute-done | bytes 884768 | tf_op jit(solution)/shard_map/ppermute | solution.py:13
  389.4 2.2 broadcast_select_fusion.2
  392.7 18.7 %collective-permute-done.3 = f32[221184]{0:T(1024)} collective-permute-done((f32[221184]{0:T(1024)}, f32[221184]{0:T(1024)}, u32[]{:S(2)}, u32[]{:S(2)}) %collective-permute-start.3) | collective-permute-done | bytes 884768 | tf_op jit(solution)/shard_map/ppermute | solution.py:13
  411.4 2.2 broadcast_select_fusion.3
  413.6 2.3 collective-permute-start.4
  416.7 17.4 %collective-permute-done.4 = f32[221184]{0:T(1024)} collective-permute-done((f32[221184]{0:T(1024)}, f32[221184]{0:T(1024)}, u32[]{:S(2)}, u32[]{:S(2)}) %collective-permute-start.4) | collective-permute-done | bytes 884768 | tf_op jit(solution)/shard_map/ppermute | solution.py:13
  436.2 2.0 fusion.40
  441.4 1.4 and_reduce_fusion
  445.4 3.2 fusion
  448.6 2.5 broadcast.320
  451.1 7.8 %scatter_fusion.1 = f32[128,64,128]{2,1,0:T(8,128)} fusion(f32[128,64,128]{2,1,0:T(8,128)} %broadcast.320, s32[44]{0:T(128)S(1)} %broadcast_subtract_fusion.1, f32[44,64,128]{2,1,0:T(8,128)} %bitcast.223), kind=kCustom, calls=%fused_computation.11 | custom fusion | flops 360448 | bytes 4325552 | tf_op jit(solution)/shard_map/scatter-add | solution.py:40
  459.2 10.1 %all_gather.15 = f32[8,64,128]{2,1,0:T(8,128)} all-gather(f32[2,64,128]{2,1,0:T(8,128)S(1)} %slice.243), channel_id=1, replica_groups=mesh['group'=4,'bulk'=32] {'group'}, dimensions={0}, use_global_device_ids=true | all-gather | bytes 327680 | tf_op jit(solution)/shard_map/all_gather | solution.py:33
  469.3 2.1 fusion.35
  471.4 15.3 %all-gather.5.cloned.1.call-done = f32[128,64,128]{2,1,0:T(8,128)} async-done(((f32[4,64,128]{2,1,0:T(8,128)}), f32[128,64,128]{2,1,0:T(8,128)}) %all-gather.5.cloned.1.call-update) | async-done | bytes 4194320 | tf_op jit(solution)/shard_map/all_gather | solution.py:39
  486.7 4.0 gather_fusion.7
  490.7 5.4 fusion.15
  496.2 73.8 %reduce-scatter.5.cloned.1.call-done = f32[4,64,128]{2,1,0:T(8,128)} async-done(((f32[128,64,128]{2,1,0:T(8,128)}), f32[4,64,128]{2,1,0:T(8,128)}) %reduce-scatter.5.cloned.1.call-update) | async-done | bytes 131088 | tf_op jit(solution)/shard_map/reduce_scatter | solution.py:41
  570.0 1.7 fusion.19
  571.6 1.6 fusion.27
  573.5 66.0 %psum.31 = f32[64,64]{1,0:T(8,128)S(1)} all-reduce(f32[64,64]{1,0:T(8,128)S(1)} %convolution_bitcast_fusion.7), channel_id=1, replica_groups=mesh['group'=4,'bulk'=32] {'group','bulk'}, use_global_device_ids=true, to_apply=%region_13.17 | all-reduce | flops 4096 | bytes 32768 | tf_op jit(solution)/shard_map/psum | solution.py:24
  639.7 5.8 cholesky.81
  646.9 4.9 custom-call.17
  653.1 1.8 fusion.22
  (102 shorter events, 41.5 us)
Async XLA Ops:
  7.2 137.9 %copy-start = (f32[2,4,128,128]{3,2,1,0:T(8,128)S(1)}, f32[2,4,128,128]{3,2,1,0:T(8,128)}, u32[]{:S(2)}) copy-start(f32[2,4,128,128]{3,2,1,0:T(8,128)} %param.29) | copy-start | bytes 1572868
  7.2 18.1 %copy-start.3 = (f32[4,64,128]{2,1,0:T(8,128)S(1)}, f32[4,64,128]{2,1,0:T(8,128)}, u32[]{:S(2)}) copy-start(f32[4,64,128]{2,1,0:T(8,128)} %param.26) | copy-start | bytes 393220
  7.2 16.2 %copy-start.2 = (s32[512]{0:T(512)S(1)}, s32[512]{0:T(512)}, u32[]{:S(2)}) copy-start(s32[512]{0:T(512)} %param.31) | copy-start | bytes 6148
  7.2 4.3 copy-start.1
  7.2 55.2 %all-gather.3.cloned.1.call-start = ((), (), s32[]{:S(2)}) async-start(), calls=%async_computation.2 | async-start | bytes 4325376 | tf_op jit(solution)/shard_map/all_gather | solution.py:39
  7.3 1.9 copy-start.11
  9.9 133.5 %reduce-scatter.3.cloned.1.call-start = ((), (), s32[]{:S(2)}) async-start(), calls=%async_computation.3 | async-start | bytes 4325376 | tf_op jit(solution)/shard_map/reduce_scatter | solution.py:41
  39.0 447.7 %all-gather.5.cloned.1.call-start = ((), (), s32[]{:S(2)}) async-start(), calls=%async_computation.4 | async-start | bytes 4325376 | tf_op jit(solution)/shard_map/all_gather | solution.py:39
  71.8 266.4 %copy-start.13 = (s32[4]{0:T(128)S(1)}, s32[4]{0:T(128)}, u32[]{:S(2)}) copy-start(s32[4]{0:T(128)} %gather_fusion.3) | copy-start | bytes 52
  146.7 0.7 copy-start.7
  334.2 2.8 copy-start.4
  337.6 3.7 collective-permute-start
  343.5 21.5 %collective-permute-start.1 = (f32[221184]{0:T(1024)}, f32[221184]{0:T(1024)}, u32[]{:S(2)}, u32[]{:S(2)}) collective-permute-start(f32[221184]{0:T(1024)} %broadcast_select_fusion), channel_id=1, source_target_pairs={{0,2},{1,3},{2,0},{3,1},{4,6},{5,7},{6,4},{7,5},{8,10},{9,11},{10,... | collective-permute-start | bytes 2654216 | tf_op jit(solution)/shard_map/ppermute | solution.py:13
  367.2 48.7 %copy-start.14 = (s32[3]{0:T(128)S(1)}, s32[3]{0:T(128)}, u32[]{:S(2)}) copy-start(s32[3]{0:T(128)} %constant.237.clone.1) | copy-start | bytes 40
  367.2 49.5 %copy-start.8 = (f32[64,4,128]{2,0,1:T(8,128)S(1)}, f32[64,4,128]{2,0,1:T(8,128)}, u32[]{:S(2)}) copy-start(f32[64,4,128]{2,0,1:T(8,128)} %fusion.73) | copy-start | bytes 393220
  367.2 22.2 %collective-permute-start.2 = (f32[221184]{0:T(1024)}, f32[221184]{0:T(1024)}, u32[]{:S(2)}, u32[]{:S(2)}) collective-permute-start(f32[221184]{0:T(1024)} %broadcast_select_fusion.1), channel_id=1, source_target_pairs={{0,4},{1,5},{2,6},{3,7},{4,0},{5,1},{6,2},{7,3},{8,12},{9,13},{10,... | collective-permute-start | bytes 2654216 | tf_op jit(solution)/shard_map/ppermute | solution.py:13
  391.6 19.8 %collective-permute-start.3 = (f32[221184]{0:T(1024)}, f32[221184]{0:T(1024)}, u32[]{:S(2)}, u32[]{:S(2)}) collective-permute-start(f32[221184]{0:T(1024)} %broadcast_select_fusion.2), channel_id=1, source_target_pairs={{0,8},{1,9},{2,10},{3,11},{4,12},{5,13},{6,14},{7,15},{8,0},{9,1},... | collective-permute-start | bytes 2654216 | tf_op jit(solution)/shard_map/ppermute | solution.py:13
  392.7 47.8 %copy-start.12 = (s32[4,11,1]{1,0,2:T(4,128)S(1)}, s32[4,11,1]{1,0,2:T(4,128)}, u32[]{:S(2)}) copy-start(s32[4,11,1]{1,0,2:T(4,128)} %get-tuple-element.98) | copy-start | bytes 532
  413.6 20.5 %collective-permute-start.4 = (f32[221184]{0:T(1024)}, f32[221184]{0:T(1024)}, u32[]{:S(2)}, u32[]{:S(2)}) collective-permute-start(f32[221184]{0:T(1024)} %broadcast_select_fusion.3), channel_id=1, source_target_pairs={{0,16},{1,17},{2,18},{3,19},{4,20},{5,21},{6,22},{7,23},{8,24},{9,... | collective-permute-start | bytes 2654216 | tf_op jit(solution)/shard_map/ppermute | solution.py:13
  435.3 0.9 copy-start.6
  438.3 0.7 copy-start.9
  438.9 131.0 %reduce-scatter.5.cloned.1.call-start = ((), (), s32[]{:S(2)}) async-start(), calls=%async_computation.5 | async-start | bytes 4325376 | tf_op jit(solution)/shard_map/reduce_scatter | solution.py:41
  440.5 4.9 copy-start.5
  496.2 158.8 %copy-start.10 = (f32[4,64,128]{2,1,0:T(8,128)S(1)}, f32[4,64,128]{2,1,0:T(8,128)}, u32[]{:S(2)}) copy-start(f32[4,64,128]{2,1,0:T(8,128)} %copy-done.9) | copy-start | bytes 393220
Sparse Core Ops, SparseCore 0:
  10.3 49.7 all-gather.2
  63.7 79.6 reduce-scatter.2
  439.1 47.6 all-gather.4
  490.2 79.7 reduce-scatter.4
where the time goes:
time: 666 us; the launch traced here: 662 us
  waiting for transfers between devices  236 us (35%)
  blocking collectives  218 us (33%)
  other arithmetic  90.6 us (14%)
  local copies, waits for them, and re-layouts  50.3 us (8%)
  matrix products  39.5 us (6%)
  between operations  18.6 us (3%)
  starting transfers between devices  8.54 us (1%)
    psum x3, blocking collectives, global_gram(): total = lax.psum(partial_gram, ('group', 'bulk'))  195 us
    reduce_scatter x2, waiting for transfers between devices, operate(): owed = lax.psum_scatter(buffer, 'bulk', scatter_dimension=0, tiled=True)  145 us
    ppermute x5, waiting for transfers between devices, from_partner(): return lax.ppermute(value, axis, pairs)  75.6 us
    another operation x9, other arithmetic, chol_apply(): factor = jnp.linalg.cholesky(matrix)  23.9 us
    all_gather x2, blocking collectives, operate(): lax.all_gather(vectors[:boundary_rows], 'group', axis=0, tiled=True)  23.1 us
    another operation x6, other arithmetic, chol_apply(): lax.linalg.triangular_solve(factor, middle, left_side=True, lower=True, t...  22.2 us
    scatter-add x2, other arithmetic, operate(): jax.ops.segment_sum(flat_terms, column_ids.reshape(-1), num_segments=grou...  15.8 us
    all_gather x2, waiting for transfers between devices, operate(): panel = lax.all_gather(vectors, 'bulk', axis=0, tiled=True)  15.3 us
  transfers between devices with their start and end apart: 9, of which 7 were waited for; matrix products, arithmetic and copies ran while one was open for 12% of the time, Pallas kernels for 0%

commit v1 on v0

--- a/solution.py
+++ b/solution.py
@@ -21,7 +21,7 @@
 
 def global_gram(left, right):
     partial_gram = jnp.einsum("snt,smt->nm", left, right, precision=highest)
-    total = lax.psum(partial_gram, ("group", "bulk"))
+    total = lax.psum(lax.psum(partial_gram, "group"), "bulk")
     return 0.5 * (total + total.T)
 
 

time: 666 us -> 894 us (1.34)
  blocking collectives: 218 us -> 440 us
    psum x3 -> x6, blocking collectives: 195 us -> 417 us  [global_gram(): total = lax.psum(lax.psum(partial_gram, 'group'), 'bulk')]
  transfers between devices with their start and end apart: 9 -> 9, of which waited for: 7 -> 7; matrix products, arithmetic and copies ran while one was open for 12% -> 9% of each run, Pallas kernels for 0% -> 0%
where the time goes in v1:
time: 894 us; the launch traced here: 886 us
  blocking collectives  440 us (49%)
  waiting for transfers between devices  241 us (27%)
  other arithmetic  90.6 us (10%)
  local copies, waits for them, and re-layouts  50.3 us (6%)
  matrix products  38.6 us (4%)
  between operations  18.6 us (2%)
    psum x6, blocking collectives, global_gram(): total = lax.psum(lax.psum(partial_gram, 'group'), 'bulk')  417 us
    reduce_scatter x2, waiting for transfers between devices, operate(): owed = lax.psum_scatter(buffer, 'bulk', scatter_dimension=0, tiled=True)  145 us
    ppermute x5, waiting for transfers between devices, from_partner(): return lax.ppermute(value, axis, pairs)  83.1 us
    another operation x9, other arithmetic, chol_apply(): factor = jnp.linalg.cholesky(matrix)  23.9 us
    all_gather x2, blocking collectives, operate(): lax.all_gather(vectors[:boundary_rows], 'group', axis=0, tiled=True)  23.3 us
    another operation x6, other arithmetic, chol_apply(): lax.linalg.triangular_solve(factor, middle, left_side=True, lower=True, t...  22.2 us
  transfers between devices with their start and end apart: 9, of which 7 were waited for; matrix products, arithmetic and copies ran while one was open for 9% of the time, Pallas kernels for 0%

profile of v1, /device:TPU:1, one launch (start us, length us, event | category | flops | bytes accessed | tf_op | source)
XLA Modules:
  0.0 885.9 jit_solution(3039968439865863156)
XLA Ops:
  7.3 1.9 copy.86
  9.9 1.6 copy.40
  12.1 2.6 scatter_custom_fusion.1
  15.9 1.5 gather_fusion
  18.7 2.2 gather_fusion.5
  25.3 3.2 fusion.4
  28.5 2.5 broadcast.320.clone
  31.0 8.0 scatter_fusion
  45.5 13.0 %all_gather.13 = f32[8,64,128]{2,1,0:T(8,128)} all-gather(f32[2,64,128]{2,1,0:T(8,128)} %slice.208), channel_id=1, replica_groups=mesh['group'=4,'bulk'=32] {'group'}, dimensions={0}, use_global_device_ids=true | all-gather | bytes 327680 | tf_op jit(solution)/shard_map/all_gather | solution.py:33
  60.9 1.5 bitcast_dynamic-update-slice_fusion
  62.4 4.0 gather_fusion.1
  66.4 5.4 fusion.12
  71.8 71.6 %reduce-scatter.3.cloned.1.call-done = f32[4,64,128]{2,1,0:T(8,128)} async-done(((f32[128,64,128]{2,1,0:T(8,128)}), f32[4,64,128]{2,1,0:T(8,128)}) %reduce-scatter.3.cloned.1.call-update) | async-done | bytes 131088 | tf_op jit(solution)/shard_map/reduce_scatter | solution.py:41
  143.4 1.7 fusion.21
  145.1 1.6 fusion.29
  148.2 14.8 %all-reduce.1 = (f32[64,64]{1,0:T(8,128)}, f32[64,64]{1,0:T(8,128)}) all-reduce(f32[64,64]{1,0:T(8,128)} %convolution_bitcast_fusion.11, f32[64,64]{1,0:T(8,128)} %convolution_bitcast_fusion.12), channel_id=1, replica_groups=mesh['group'=4,'bulk'=32] {'group'}, use_global_device_ids=true, to_apply=%region_6.8 | all-reduce | flops 8192 | bytes 65536 | tf_op jit(solution)/shard_map/psum | solution.py:24
  163.0 125.0 %all-reduce = (f32[64,64]{1,0:T(8,128)}, f32[64,64]{1,0:T(8,128)}) all-reduce(f32[64,64]{1,0:T(8,128)} %get-tuple-element.93, f32[64,64]{1,0:T(8,128)} %get-tuple-element.94), channel_id=1, replica_groups=mesh['group'=4,'bulk'=32] {'bulk'}, use_global_device_ids=true, to_apply=%region_7.9 | all-reduce | flops 8192 | bytes 65536 | tf_op jit(solution)/shard_map/psum | solution.py:24
  288.0 1.4 copy.45
  289.5 1.4 fusion.56
  290.9 1.4 copy.48
  292.3 1.5 copy.43
  293.8 1.4 fusion.61
  295.1 1.4 copy.44
  296.6 1.4 fusion.60
  298.0 7.2 cholesky.59
  306.7 2.1 fusion.36
  308.7 6.3 custom-call.13
  317.0 1.8 fusion.25
  319.8 1.4 fusion.55
  321.2 7.2 cholesky.70
  329.9 2.1 fusion.37
  331.9 6.3 custom-call.15
  338.2 1.8 convolution_bitcast_fusion.9
  340.0 12.1 %psum.60 = f32[64,64]{1,0:T(8,128)} all-reduce(f32[64,64]{1,0:T(8,128)} %convolution_bitcast_fusion.9), channel_id=1, replica_groups=mesh['group'=4,'bulk'=32] {'group'}, use_global_device_ids=true, to_apply=%region_10.14 | all-reduce | flops 4096 | bytes 32768 | tf_op jit(solution)/shard_map/psum | solution.py:24
  352.1 127.8 %psum.61 = f32[64,64]{1,0:T(8,128)} all-reduce(f32[64,64]{1,0:T(8,128)} %psum.60), channel_id=1, replica_groups=mesh['group'=4,'bulk'=32] {'bulk'}, use_global_device_ids=true, to_apply=%region_11.15 | all-reduce | flops 4096 | bytes 32768 | tf_op jit(solution)/shard_map/psum | solution.py:24
  479.9 1.4 copy.49
  484.6 1.4 bitcast_dynamic-update-slice_fusion.3
  486.0 1.4 bitcast_dynamic-update-slice_fusion.2
  488.0 5.7 collective-permute-start
  496.7 2.2 broadcast_select_fusion
  498.9 21.5 %collective-permute-done.1 = f32[221184]{0:T(1024)} collective-permute-done((f32[221184]{0:T(1024)}, f32[221184]{0:T(1024)}, u32[]{:S(2)}, u32[]{:S(2)}) %collective-permute-start.1) | collective-permute-done | bytes 884768 | tf_op jit(solution)/shard_map/ppermute | solution.py:13
  520.4 2.2 broadcast_select_fusion.1
  522.7 22.2 %collective-permute-done.2 = f32[221184]{0:T(1024)} collective-permute-done((f32[221184]{0:T(1024)}, f32[221184]{0:T(1024)}, u32[]{:S(2)}, u32[]{:S(2)}) %collective-permute-start.2) | collective-permute-done | bytes 884768 | tf_op jit(solution)/shard_map/ppermute | solution.py:13
  544.8 2.2 broadcast_select_fusion.2
  547.0 19.8 %collective-permute-done.3 = f32[221184]{0:T(1024)} collective-permute-done((f32[221184]{0:T(1024)}, f32[221184]{0:T(1024)}, u32[]{:S(2)}, u32[]{:S(2)}) %collective-permute-start.3) | collective-permute-done | bytes 884768 | tf_op jit(solution)/shard_map/ppermute | solution.py:13
  566.8 2.2 broadcast_select_fusion.3
  569.8 19.7 %collective-permute-done.4 = f32[221184]{0:T(1024)} collective-permute-done((f32[221184]{0:T(1024)}, f32[221184]{0:T(1024)}, u32[]{:S(2)}, u32[]{:S(2)}) %collective-permute-start.4) | collective-permute-done | bytes 884768 | tf_op jit(solution)/shard_map/ppermute | solution.py:13
  591.7 2.0 fusion.40
  596.6 1.4 and_reduce_fusion
  600.6 3.2 fusion
  603.8 2.5 broadcast.320
  606.3 7.8 scatter_fusion.1
  614.4 10.3 %all_gather.15 = f32[8,64,128]{2,1,0:T(8,128)} all-gather(f32[2,64,128]{2,1,0:T(8,128)S(1)} %slice.243), channel_id=1, replica_groups=mesh['group'=4,'bulk'=32] {'group'}, dimensions={0}, use_global_device_ids=true | all-gather | bytes 327680 | tf_op jit(solution)/shard_map/all_gather | solution.py:33
  624.7 2.1 fusion.35
  626.8 12.9 %all-gather.5.cloned.1.call-done = f32[128,64,128]{2,1,0:T(8,128)} async-done(((f32[4,64,128]{2,1,0:T(8,128)}), f32[128,64,128]{2,1,0:T(8,128)}) %all-gather.5.cloned.1.call-update) | async-done | bytes 4194320 | tf_op jit(solution)/shard_map/all_gather | solution.py:39
  639.7 4.0 gather_fusion.7
  643.7 5.4 fusion.15
  649.1 73.8 %reduce-scatter.5.cloned.1.call-done = f32[4,64,128]{2,1,0:T(8,128)} async-done(((f32[128,64,128]{2,1,0:T(8,128)}), f32[4,64,128]{2,1,0:T(8,128)}) %reduce-scatter.5.cloned.1.call-update) | async-done | bytes 131088 | tf_op jit(solution)/shard_map/reduce_scatter | solution.py:41
  723.0 1.7 fusion.19
  724.6 1.6 fusion.27
  726.5 13.2 %psum.62 = f32[64,64]{1,0:T(8,128)S(1)} all-reduce(f32[64,64]{1,0:T(8,128)S(1)} %convolution_bitcast_fusion.7), channel_id=1, replica_groups=mesh['group'=4,'bulk'=32] {'group'}, use_global_device_ids=true, to_apply=%region_16.20 | all-reduce | flops 4096 | bytes 32768 | tf_op jit(solution)/shard_map/psum | solution.py:24
  739.7 124.3 %psum.63 = f32[64,64]{1,0:T(8,128)S(1)} all-reduce(f32[64,64]{1,0:T(8,128)S(1)} %psum.62), channel_id=1, replica_groups=mesh['group'=4,'bulk'=32] {'bulk'}, use_global_device_ids=true, to_apply=%region_17.21 | all-reduce | flops 4096 | bytes 32768 | tf_op jit(solution)/shard_map/psum | solution.py:24
  864.2 5.8 cholesky.81
  871.4 4.9 custom-call.17
  (107 shorter events, 40.6 us)
Async XLA Ops:
  7.2 137.9 %copy-start = (f32[2,4,128,128]{3,2,1,0:T(8,128)S(1)}, f32[2,4,128,128]{3,2,1,0:T(8,128)}, u32[]{:S(2)}) copy-start(f32[2,4,128,128]{3,2,1,0:T(8,128)} %param.29) | copy-start | bytes 1572868
  7.2 18.1 %copy-start.3 = (f32[4,64,128]{2,1,0:T(8,128)S(1)}, f32[4,64,128]{2,1,0:T(8,128)}, u32[]{:S(2)}) copy-start(f32[4,64,128]{2,1,0:T(8,128)} %param.26) | copy-start | bytes 393220
  7.2 16.2 %copy-start.2 = (s32[512]{0:T(512)S(1)}, s32[512]{0:T(512)}, u32[]{:S(2)}) copy-start(s32[512]{0:T(512)} %param.31) | copy-start | bytes 6148
  7.2 4.3 copy-start.1
  7.2 55.2 %all-gather.3.cloned.1.call-start = ((), (), s32[]{:S(2)}) async-start(), calls=%async_computation.2 | async-start | bytes 4325376 | tf_op jit(solution)/shard_map/all_gather | solution.py:39
  7.3 1.9 copy-start.12
  9.9 133.5 %reduce-scatter.3.cloned.1.call-start = ((), (), s32[]{:S(2)}) async-start(), calls=%async_computation.3 | async-start | bytes 4325376 | tf_op jit(solution)/shard_map/reduce_scatter | solution.py:41
  39.0 600.7 %all-gather.5.cloned.1.call-start = ((), (), s32[]{:S(2)}) async-start(), calls=%async_computation.4 | async-start | bytes 4325376 | tf_op jit(solution)/shard_map/all_gather | solution.py:39
  71.8 421.8 %copy-start.14 = (s32[4]{0:T(128)S(1)}, s32[4]{0:T(128)}, u32[]{:S(2)}) copy-start(s32[4]{0:T(128)} %gather_fusion.3) | copy-start | bytes 52
  146.7 0.7 copy-start.8
  484.6 2.8 copy-start.4
  488.0 8.7 collective-permute-start
  498.9 21.5 %collective-permute-start.1 = (f32[221184]{0:T(1024)}, f32[221184]{0:T(1024)}, u32[]{:S(2)}, u32[]{:S(2)}) collective-permute-start(f32[221184]{0:T(1024)} %broadcast_select_fusion), channel_id=1, source_target_pairs={{0,2},{1,3},{2,0},{3,1},{4,6},{5,7},{6,4},{7,5},{8,10},{9,11},{10,... | collective-permute-start | bytes 2654216 | tf_op jit(solution)/shard_map/ppermute | solution.py:13
  522.6 46.4 %copy-start.15 = (s32[3]{0:T(128)S(1)}, s32[3]{0:T(128)}, u32[]{:S(2)}) copy-start(s32[3]{0:T(128)} %constant.237.clone.1) | copy-start | bytes 40
  522.6 47.2 %copy-start.9 = (f32[64,4,128]{2,0,1:T(8,128)S(1)}, f32[64,4,128]{2,0,1:T(8,128)}, u32[]{:S(2)}) copy-start(f32[64,4,128]{2,0,1:T(8,128)} %fusion.73) | copy-start | bytes 393220
  522.6 22.2 %collective-permute-start.2 = (f32[221184]{0:T(1024)}, f32[221184]{0:T(1024)}, u32[]{:S(2)}, u32[]{:S(2)}) collective-permute-start(f32[221184]{0:T(1024)} %broadcast_select_fusion.1), channel_id=1, source_target_pairs={{0,4},{1,5},{2,6},{3,7},{4,0},{5,1},{6,2},{7,3},{8,12},{9,13},{10,... | collective-permute-start | bytes 2654216 | tf_op jit(solution)/shard_map/ppermute | solution.py:13
  547.0 19.8 %collective-permute-start.3 = (f32[221184]{0:T(1024)}, f32[221184]{0:T(1024)}, u32[]{:S(2)}, u32[]{:S(2)}) collective-permute-start(f32[221184]{0:T(1024)} %broadcast_select_fusion.2), channel_id=1, source_target_pairs={{0,8},{1,9},{2,10},{3,11},{4,12},{5,13},{6,14},{7,15},{8,0},{9,1},... | collective-permute-start | bytes 2654216 | tf_op jit(solution)/shard_map/ppermute | solution.py:13
  547.0 48.7 %copy-start.13 = (s32[4,11,1]{1,0,2:T(4,128)S(1)}, s32[4,11,1]{1,0,2:T(4,128)}, u32[]{:S(2)}) copy-start(s32[4,11,1]{1,0,2:T(4,128)} %get-tuple-element.100) | copy-start | bytes 532
  569.0 20.5 %collective-permute-start.4 = (f32[221184]{0:T(1024)}, f32[221184]{0:T(1024)}, u32[]{:S(2)}, u32[]{:S(2)}) collective-permute-start(f32[221184]{0:T(1024)} %broadcast_select_fusion.3), channel_id=1, source_target_pairs={{0,16},{1,17},{2,18},{3,19},{4,20},{5,21},{6,22},{7,23},{8,24},{9,... | collective-permute-start | bytes 2654216 | tf_op jit(solution)/shard_map/ppermute | solution.py:13
  590.8 0.9 copy-start.7
  593.7 0.7 copy-start.10
  594.4 128.6 %reduce-scatter.5.cloned.1.call-start = ((), (), s32[]{:S(2)}) async-start(), calls=%async_computation.5 | async-start | bytes 4325376 | tf_op jit(solution)/shard_map/reduce_scatter | solution.py:41
  595.7 4.9 copy-start.5
  649.1 228.4 %copy-start.6 = (f32[4,64,128]{2,1,0:T(8,128)S(1)}, f32[4,64,128]{2,1,0:T(8,128)}, u32[]{:S(2)}) copy-start(f32[4,64,128]{2,1,0:T(8,128)} %get-tuple-element.97) | copy-start | bytes 393220
  649.1 229.3 %copy-start.11 = (f32[4,64,128]{2,1,0:T(8,128)S(1)}, f32[4,64,128]{2,1,0:T(8,128)}, u32[]{:S(2)}) copy-start(f32[4,64,128]{2,1,0:T(8,128)} %copy-done.10) | copy-start | bytes 393220
Sparse Core Ops, SparseCore 0:
  10.3 49.7 all-gather.2
  63.7 79.6 reduce-scatter.2
  594.5 45.1 all-gather.4
  643.2 79.7 reduce-scatter.4
